TPU v7x, 32 devices: a whole 2x2x4 slice. The times are simulated.
32 devices in a mesh: run: 1, row: 16 (over z, y, core), col: 1, seg: 2 (over x).
Axes of the slice: x: 2, y: 2, z: 4, core: 2. Of those that a mesh axis runs over, the one named last changes fastest.
Arguments:
- traces: bfloat16 [2, 1024, 2048], P(('run', 'seg'), 'row', 'col'), may hold values from -30 to 30
- live_mask: int32 [1024], P(('run', 'row')), may hold values 0 or 1
- sources: int32 [64], replicated, may hold values from 0 to 1023
- owners: int32 [64, 1], replicated, may hold values from 0 to 15; in each aligned block of 64 rows (0 to 63, 64 to 127, ...) at most 12 rows name the same one
Outputs:
- gathers: bfloat16 [192, 16, 64, 256], P(('run', 'row'), None, ('col', 'seg'))
Inputs may be any that keep to these rules, and one draw needn't show every extreme that they name: `owners`: at most 12 sources share an owner, and some owner has exactly 12.
All inputs are finite; a program needn't handle non-finite values. No bound on the sum of `live_mask` on one device may be relied on, other than what follows from the above.
Results may differ from a plain program's by a relative error of at most 0.024.
Values may be sent and summed in bfloat16 or wider, within the bound.
No kernel may reach another device: no remote copies, remote signals or barrier semaphores. Data moves between devices by JAX's collectives and lax.ppermute only.
A program may use at most 64 MiB of HBM per device.

v0:
```python
import math
import jax
import jax.numpy as jnp
from jax import lax
from jax.sharding import PartitionSpec as P

NT = 2048
NF = 1024
LAGS = 256
BAND = 64
two_pi = 2.0 * math.pi


def turn_table(first_ids, second_ids, period):
    product = first_ids[:, None] * second_ids[None, :] % period
    return product.astype(jnp.float32) * (two_pi / period)


def lag_matrix(bin_ids):
    lag_ids = jnp.arange(LAGS, dtype=jnp.int32) - LAGS // 2 + NT
    lag_angles = turn_table(bin_ids, lag_ids, NT)
    return jnp.concatenate(
        [jnp.cos(lag_angles).astype(jnp.bfloat16), -jnp.sin(lag_angles).astype(jnp.bfloat16)],
        axis=0,
    )


def correlate(recv_real, recv_imag, real_source, imag_source, lag_table):
    cross_real = (
        real_source[:, None, :] * recv_real[:, :, None]
        + imag_source[:, None, :] * recv_imag[:, :, None]
    ).astype(jnp.bfloat16)
    cross_imag = (
        imag_source[:, None, :] * recv_real[:, :, None]
        - real_source[:, None, :] * recv_imag[:, :, None]
    ).astype(jnp.bfloat16)
    stacked_cross = jnp.concatenate([cross_real, cross_imag], axis=0)
    return jnp.einsum("fl,fgv->gvl", lag_table, stacked_cross, preferred_element_type=jnp.float32)


def local(traces, live_mask, sources, owners):
    col_count = lax.axis_size("col")
    seg_count = lax.axis_size("seg")
    row_count = lax.axis_size("row")
    samples = traces[0]
    channels = samples.shape[0]
    local_width = samples.shape[1]
    num_sources = sources.shape[0]
    first_sample = lax.axis_index("col") * local_width
    half_bins = NF // col_count
    sample_ids = first_sample + jnp.arange(local_width, dtype=jnp.int32)
    bin_ids = jnp.arange(half_bins * lax.axis_size("col"), dtype=jnp.int32)
    angles = turn_table(sample_ids, bin_ids, NT)
    cosine = jnp.cos(angles).astype(jnp.bfloat16)
    sine_table = jnp.sin(angles).astype(jnp.bfloat16)
    real_part = jnp.einsum("tf,ct->fc", cosine, samples, preferred_element_type=jnp.float32)
    imag_part = -jnp.einsum("tf,ct->fc", sine_table, samples, preferred_element_type=jnp.float32)
    spectra = lax.psum_scatter(
        jnp.concatenate([real_part, imag_part], axis=1).astype(jnp.bfloat16),
        "col",
        scatter_dimension=0,
        tiled=True,
    ).astype(jnp.float32)
    squares = (spectra * spectra).reshape(half_bins // BAND, BAND, 2, channels)
    band_power = jnp.sum(squares, axis=(1, 2)) / (2 * BAND) + 1e-05
    scaling = live_mask.astype(jnp.float32)[None, :] / jnp.sqrt(band_power)
    scaling = jnp.repeat(scaling, BAND, axis=0)
    whitened = (
        (spectra.reshape(half_bins, 2, channels) * scaling[:, None, :])
        .reshape(half_bins, 2 * channels)
        .astype(jnp.bfloat16)
    )
    white_real = whitened[:, :channels]
    white_imag = whitened[:, channels:]
    everyone = lax.all_gather(whitened, "row", axis=1, tiled=True)
    block_ids = sources // channels
    within = sources % channels
    real_cols = block_ids * (2 * channels) + within
    source_real = jnp.take(everyone, real_cols, axis=1)
    source_imag = jnp.take(everyone, real_cols + channels, axis=1)
    receivers = channels // (col_count * seg_count)
    bin_ids = lax.axis_index("col") * half_bins + jnp.arange(half_bins, dtype=jnp.int32)
    lag_table = lag_matrix(bin_ids)
    real_source = source_real.astype(jnp.float32)
    imag_source = source_imag.astype(jnp.float32)

    def one_group(offset):
        recv_real = lax.dynamic_slice_in_dim(white_real, offset, receivers, 1).astype(jnp.float32)
        recv_imag = lax.dynamic_slice_in_dim(white_imag, offset, receivers, 1).astype(jnp.float32)
        return correlate(recv_real, recv_imag, real_source, imag_source, lag_table)

    offsets = (
        jnp.arange(receivers * lax.axis_size(("col", "seg")) // receivers, dtype=jnp.int32)
        * receivers
    )
    blocks = lax.map(one_group, offsets)
    stacked = lax.psum_scatter(
        blocks.reshape(receivers * lax.axis_size(("col", "seg")), num_sources, LAGS).astype(
            jnp.bfloat16
        ),
        ("col", "seg"),
        scatter_dimension=0,
        tiled=True,
    ).astype(jnp.float32)
    mean_sq = jnp.mean(stacked * stacked, axis=-1, keepdims=True)
    normed = (stacked / jnp.sqrt(mean_sq + 1e-06)).astype(jnp.bfloat16)
    capacity = 3 * num_sources // row_count
    owner_ids = owners[:, 0]
    order_ids = jnp.arange(num_sources, dtype=jnp.int32)
    earlier = (owner_ids[:, None] == owner_ids[None, :]) & (order_ids[None, :] < order_ids[:, None])
    slot_rank = jnp.sum(earlier.astype(jnp.int32), axis=1)
    slot_ids = owner_ids * capacity + slot_rank
    placing = (
        jnp.arange(row_count * capacity, dtype=jnp.int32)[:, None] == slot_ids[None, :]
    ).astype(jnp.bfloat16)
    outgoing = jnp.einsum(
        "sv,gvl->sgl", placing, normed, preferred_element_type=jnp.float32
    ).astype(jnp.bfloat16)
    return lax.all_to_all(outgoing[:, None], "row", split_axis=0, concat_axis=1, tiled=True)


def solution(mesh):
    placed = (P(("run", "seg"), "row", "col"), P(("run", "row")), P(), P())
    return jax.shard_map(
        local,
        mesh=mesh,
        in_specs=placed,
        out_specs=P(("run", "row"), None, ("col", "seg"), None),
        check_vma=False,
    )
```

profile of v0, /device:TPU:1, one launch (start us, length us, event | category | flops | bytes accessed | tf_op | source)
XLA Modules:
  0.0 271.0 jit_solution(1408020758581116476)
XLA Ops:
  6.5 0.9 copy-done
  7.5 31.3 %fusion.21 = bf16[1024,64]{0,1:T(8,128)(2,1)S(1)} fusion(bf16[1,64,2048]{2,1,0:T(8,128)(2,1)S(1)} %copy-done), kind=kOutput, calls=%fused_computation.35 | convolution fusion | flops 300023808 | bytes 393216 | tf_op jit(solution)/shard_map/tf,ct->fc/dot_general | solution.py:57
  38.8 31.2 %fusion.22 = bf16[1024,64]{0,1:T(8,128)(2,1)S(1)} fusion(bf16[1,64,2048]{2,1,0:T(8,128)(2,1)S(1)} %copy-done), kind=kOutput, calls=%fused_computation.36 | convolution fusion | flops 299958272 | bytes 393216 | tf_op jit(solution)/shard_map/tf,ct->fc/dot_general | solution.py:56
  70.1 0.3 mul.149
  70.4 0.2 reduce_sum.28
  70.7 0.1 copy.16
  70.8 0.2 broadcast_in_dim.19
  71.0 0.2 mul.150
  71.2 0.8 multiply_convert_fusion
  72.1 1.0 fusion.48
  73.1 4.2 %cosine_convert_fusion.4 = bf16[1024,256]{1,0:T(8,128)(2,1)S(1)} fusion(s32[256]{0:T(256)S(1)} %iota_add_fusion), kind=kLoop, calls=%fused_computation.43 | loop fusion | flops 3932160 | bytes 525312 | tf_op jit(solution)/shard_map/convert_element_type | solution.py:23
  77.3 4.0 %fusion.31 = bf16[1024,256]{1,0:T(8,128)(2,1)S(1)} fusion(s32[256]{0:T(256)S(1)} %iota_add_fusion), kind=kLoop, calls=%fused_computation.47 | loop fusion | flops 4718592 | bytes 525312 | tf_op jit(solution)/shard_map/neg | solution.py:23
  81.4 1.0 pad_maximum_fusion
  82.4 42.7 %all-gather.2.cloned.1.call-done = bf16[1024,2048]{0,1:T(8,128)(2,1)} async-done(((bf16[1024,128]{0,1:T(8,128)(2,1)}), bf16[1024,2048]{0,1:T(8,128)(2,1)}) %all-gather.2.cloned.1.call-update) | async-done | bytes 4194320 | tf_op jit(solution)/shard_map/all_gather | solution.py:75
  125.1 3.5 %gather_fusion = bf16[64,1024]{1,0:T(8,128)(2,1)S(1)} fusion(bf16[1024,2048]{0,1:T(8,128)(2,1)} %all-gather.2.cloned.1.call-done, s32[1024]{0:T(1024)S(1)} %pad_clamp_fusion.1), kind=kCustom, calls=%fused_computation.clone | custom fusion | bytes 262400 | tf_op jit(solution)/shard_map/jit(_take)/gather | solution.py:79
  128.6 3.5 %gather_fusion.1 = bf16[64,1024]{1,0:T(8,128)(2,1)S(1)} fusion(bf16[1024,2048]{0,1:T(8,128)(2,1)} %all-gather.2.cloned.1.call-done, s32[1024]{0:T(1024)S(1)} %pad_clamp_fusion), kind=kCustom, calls=%fused_computation.1.clone | custom fusion | bytes 262400 | tf_op jit(solution)/shard_map/jit(_take)/gather | solution.py:80
  132.2 0.1 bitcast_convert_fusion
  132.3 16.3 %while.10 = (s32[]{:T(128)}, bf16[2,32,64,256]{3,2,1,0:T(8,128)(2,1)S(1)}, f32[1024,64]{0,1:T(8,128)S(1)}, s32[2]{0:T(128)S(1)}, bf16[1024,64]{0,1:T(8,128)(2,1)...) while((s32[]{:T(128)}, ...), condition=%wide.region_3.5_spmd, body=%wide.region_2.4_spmd.sunk | while | flops 2181103616 | bytes 25297088 | solution.py:96
  132.3 0.7 dynamic_slice.15
  135.1 2.8 %add_convert_fusion.2 = (bf16[1024,32,64]{0,2,1:T(8,128)(2,1)S(1)}, bf16[1024,32,64]{0,2,1:T(8,128)(2,1)S(1)}) fusion(f32[1024,32]{0,1:T(8,128)S(1)} %get-tuple-element.129, f32[1024,64]{0,1:T(8,128)S(1)} %get-tuple-element.160, f32[1024,32]{0,1:T(8,128)S(1)} %get-tuple-element.130, f32[1024,64]{0,1:T(8,128)S(1)} %get-tuple-element.157), kind=kLoop, calls=%fused_computation.7.clone.1 | loop fusion | flops 16777216 | bytes 9175040 | tf_op jit(solution)/shard_map/while/body/eval_jaxpr/convert_element_type | solution.py:32
  137.9 2.5 bitcast_dynamic-update-slice_fusion.2
  140.5 0.7 dynamic_slice.15
  143.3 2.8 %add_convert_fusion.2 = (bf16[1024,32,64]{0,2,1:T(8,128)(2,1)S(1)}, bf16[1024,32,64]{0,2,1:T(8,128)(2,1)S(1)}) fusion(f32[1024,32]{0,1:T(8,128)S(1)} %get-tuple-element.129, f32[1024,64]{0,1:T(8,128)S(1)} %get-tuple-element.160, f32[1024,32]{0,1:T(8,128)S(1)} %get-tuple-element.130, f32[1024,64]{0,1:T(8,128)S(1)} %get-tuple-element.157), kind=kLoop, calls=%fused_computation.7.clone.1 | loop fusion | flops 16777216 | bytes 9175040 | tf_op jit(solution)/shard_map/while/body/eval_jaxpr/convert_element_type | solution.py:32
  146.1 2.5 bitcast_dynamic-update-slice_fusion.2
  148.7 1.3 copy-done.1
  150.0 0.2 convert_reduce_fusion
  150.2 29.8 %reduce-scatter.2.cloned.1.call-done = bf16[32,64,256]{2,1,0:T(8,128)(2,1)} async-done(((bf16[64,64,256]{2,1,0:T(8,128)(2,1)}), bf16[32,64,256]{2,1,0:T(8,128)(2,1)}) %reduce-scatter.2.cloned.1.call-update) | async-done | bytes 1048592 | tf_op jit(solution)/shard_map/reduce_scatter | solution.py:97
  180.0 1.6 fusion.18
  181.6 2.3 convert_bitcast_fusion
  184.0 1.8 copy.17
  185.7 76.3 %all_to_all.18 = bf16[192,1,32,256]{3,2,1,0:T(8,128)(2,1)S(1)} all-to-all(bf16[192,1,32,256]{3,2,1,0:T(8,128)(2,1)S(1)} %copy.17), channel_id=1, replica_groups=mesh['run'=1,'row'=16,'col'=1,'seg'=2] {'row'}, dimensions={0} | all-to-all | bytes 6291456 | tf_op jit(solution)/shard_map/all_to_all | solution.py:119
  262.1 2.1 copy.18
  (32 shorter events, 0.4 us)
Async XLA Ops:
  6.5 1.0 copy-start
  6.5 118.6 %all-gather.2.cloned.1.call-start = ((), (), s32[]{:S(2)}) async-start(), calls=%async_computation.2 | async-start | bytes 4456448 | tf_op jit(solution)/shard_map/all_gather | solution.py:75
  38.8 31.9 %copy-start.4 = (s32[64]{0:T(128)S(1)}, s32[64]{0:T(128)}, u32[]{:S(2)}) copy-start(s32[64]{0:T(128)} %param.9) | copy-start | bytes 772
  70.1 2.0 copy-start.3
  72.0 108.0 %reduce-scatter.2.cloned.1.call-start = ((), (), s32[]{:S(2)}) async-start(), calls=%async_computation.3 | async-start | bytes 3145728 | tf_op jit(solution)/shard_map/reduce_scatter | solution.py:97
  132.3 17.7 %copy-start.5 = (s32[64,1]{0,1:T(1,128)S(1)}, s32[64,1]{0,1:T(1,128)}, u32[]{:S(2)}) copy-start(s32[64,1]{0,1:T(1,128)} %param.11) | copy-start | bytes 772
  135.1 2.8 %copy-start.2 = (bf16[2048,256]{1,0:T(8,128)(2,1)S(1)}, bf16[2048,256]{1,0:T(8,128)(2,1)}, u32[]{:S(2)}) copy-start(bf16[2048,256]{1,0:T(8,128)(2,1)} %get-tuple-element.162) | copy-start | bytes 3145732 | tf_op jit(solution)/shard_map/while
  143.3 2.8 %copy-start.2 = (bf16[2048,256]{1,0:T(8,128)(2,1)S(1)}, bf16[2048,256]{1,0:T(8,128)(2,1)}, u32[]{:S(2)}) copy-start(bf16[2048,256]{1,0:T(8,128)(2,1)} %get-tuple-element.162) | copy-start | bytes 3145732 | tf_op jit(solution)/shard_map/while
  148.7 1.3 copy-start.1
Sparse Core Ops, SparseCore 0:
  72.1 52.9 all-gather.1
  150.1 29.8 reduce-scatter.1
where the time goes:
time: 271 us
  blocking collectives  76.3 us (28%)
  waiting for transfers between devices  72.6 us (27%)
  matrix products  70 us (26%)
  other arithmetic  17.9 us (7%)
  local copies, waits for them, and re-layouts  16.3 us (6%)
  between operations  13.6 us (5%)
  loops' own time  4.26 us (2%)
    all_to_all x1, blocking collectives, local(): lax.all_to_all(outgoing[:, None], 'row', split_axis=0, concat_axis=1, til...  76.3 us
    all_gather x1, waiting for transfers between devices, local(): everyone = lax.all_gather(whitened, 'row', axis=1, tiled=True)  42.7 us
    dot_general x1, matrix products, local(): jnp.einsum('tf,ct->fc', sine_table, samples, preferred_element_type=jnp.f...  31.3 us
    dot_general x1, matrix products, local(): jnp.einsum('tf,ct->fc', cosine, samples, preferred_element_type=jnp.float32)  31.2 us
    reduce_scatter x1, waiting for transfers between devices, local(): lax.psum_scatter(blocks.reshape(receivers * lax.axis_size(('col', 'seg'))...  29.8 us
    convert_element_type x2, other arithmetic, correlate(): cross_real = (real_source[:, None, :] * recv_real[:, :, None] + imag_sour...  5.58 us
  transfers between devices with their start and end apart: 2, of which 2 were waited for; matrix products, arithmetic and copies ran while one was open for 4% of the time, Pallas kernels for 0%

commit v1 on v0

--- a/solution.py
+++ b/solution.py
@@ -72,7 +72,15 @@
     )
     white_real = whitened[:, :channels]
     white_imag = whitened[:, channels:]
-    everyone = lax.all_gather(whitened, "row", axis=1, tiled=True)
+    ways, here = (lax.axis_size("row"), lax.axis_index("row"))
+    grown, reach = (whitened, 1)
+    while reach < ways:
+        theirs = lax.ppermute(grown, "row", [(d, d ^ reach) for d in range(ways)])
+        mine_first = jnp.concatenate([grown, theirs], axis=1)
+        theirs_first = jnp.concatenate([theirs, grown], axis=1)
+        grown = jnp.where(here & reach == 0, mine_first, theirs_first)
+        reach = 2 * reach
+    everyone = grown
     block_ids = sources // channels
     within = sources % channels
     real_cols = block_ids * (2 * channels) + within

time: 271 us -> 361 us (1.33)
  waiting for transfers between devices: 72.6 us -> 150 us
  other arithmetic: 17.9 us -> 25.2 us
  starting transfers between devices: 0.04 us -> 5.85 us
    ppermute x0 -> x4, waiting for transfers between devices: none -> 117 us  [local(): theirs = lax.ppermute(grown, 'row', [(d, d ^ reach) for d in range(ways)])]
    all_gather x1 -> x0, waiting for transfers between devices: 42.7 us -> none  [local(): everyone = lax.all_gather(whitened, 'row', axis=1, tiled=True)]
    select_n x0 -> x4, other arithmetic: none -> 8.03 us  [local(): grown = jnp.where(here & reach == 0, mine_first, theirs_first)]
    ppermute x0 -> x4, starting transfers between devices: none -> 5.84 us  [local(): theirs = lax.ppermute(grown, 'row', [(d, d ^ reach) for d in range(ways)])]
  transfers between devices with their start and end apart: 2 -> 5, of which waited for: 2 -> 5; matrix products, arithmetic and copies ran while one was open for 4% -> 3% of each run, Pallas kernels for 0% -> 0%
where the time goes in v1:
time: 361 us
  waiting for transfers between devices  150 us (42%)
  blocking collectives  76.3 us (21%)
  matrix products  70 us (19%)
  other arithmetic  25.2 us (7%)
  local copies, waits for them, and re-layouts  16.3 us (5%)
  between operations  13.7 us (4%)
  starting transfers between devices  5.85 us (2%)
  loops' own time  3.99 us (1%)
    ppermute x4, waiting for transfers between devices, local(): theirs = lax.ppermute(grown, 'row', [(d, d ^ reach) for d in range(ways)])  117 us
    all_to_all x1, blocking collectives, local(): lax.all_to_all(outgoing[:, None], 'row', split_axis=0, concat_axis=1, til...  76.3 us
    reduce_scatter x1, waiting for transfers between devices, local(): lax.psum_scatter(blocks.reshape(receivers * lax.axis_size(('col', 'seg'))...  33 us
    dot_general x1, matrix products, local(): jnp.einsum('tf,ct->fc', sine_table, samples, preferred_element_type=jnp.f...  31.3 us
    dot_general x1, matrix products, local(): jnp.einsum('tf,ct->fc', cosine, samples, preferred_element_type=jnp.float32)  31.2 us
    select_n x4, other arithmetic, local(): grown = jnp.where(here & reach == 0, mine_first, theirs_first)  8.03 us
  transfers between devices with their start and end apart: 5, of which 5 were waited for; matrix products, arithmetic and copies ran while one was open for 3% of the time, Pallas kernels for 0%

profile of v1, /device:TPU:1, one launch (start us, length us, event | category | flops | bytes accessed | tf_op | source)
XLA Modules:
  0.0 360.9 jit_solution(9962822500371504599)
XLA Ops:
  6.5 0.9 copy-done
  7.5 31.3 %fusion.21 = bf16[1024,64]{0,1:T(8,128)(2,1)S(1)} fusion(bf16[1,64,2048]{2,1,0:T(8,128)(2,1)S(1)} %copy-done), kind=kOutput, calls=%fused_computation.37 | convolution fusion | flops 300023808 | bytes 393216 | tf_op jit(solution)/shard_map/tf,ct->fc/dot_general | solution.py:57
  38.8 31.2 %fusion.22 = bf16[1024,64]{0,1:T(8,128)(2,1)S(1)} fusion(bf16[1,64,2048]{2,1,0:T(8,128)(2,1)S(1)} %copy-done), kind=kOutput, calls=%fused_computation.38 | convolution fusion | flops 299958272 | bytes 393216 | tf_op jit(solution)/shard_map/tf,ct->fc/dot_general | solution.py:56
  71.3 1.5 collective-permute-done
  73.0 2.4 collective-permute-start.1
  75.4 11.9 %collective-permute-done.1 = bf16[1024,256]{0,1:T(8,128)(2,1)S(1)} collective-permute-done((bf16[1024,256]{0,1:T(8,128)(2,1)S(1)}, bf16[1024,256]{0,1:T(8,128)(2,1)S(1)}, u32[]{:S(2)}, u32[]{:S(2)}) %collective-permute-start.1) | collective-permute-done | bytes 524320 | tf_op jit(solution)/shard_map/ppermute | solution.py:78
  87.8 1.3 collective-permute-start.2
  89.1 22.6 %collective-permute-done.2 = bf16[1024,512]{0,1:T(8,128)(2,1)} collective-permute-done((bf16[1024,512]{0,1:T(8,128)(2,1)S(1)}, bf16[1024,512]{0,1:T(8,128)(2,1)}, u32[]{:S(2)}, u32[]{:S(2)}) %collective-permute-start.2) | collective-permute-done | bytes 1048608 | tf_op jit(solution)/shard_map/ppermute | solution.py:78
  111.8 2.5 maximum_select_fusion.1
  114.3 2.0 collective-permute-start.3
  116.4 1.0 fusion.48
  117.4 4.0 %cosine_convert_fusion.4 = bf16[1024,256]{1,0:T(8,128)(2,1)S(1)} fusion(s32[256]{0:T(256)S(1)} %iota_add_fusion), kind=kLoop, calls=%fused_computation.46 | loop fusion | flops 3932160 | bytes 525312 | tf_op jit(solution)/shard_map/convert_element_type | solution.py:23
  121.4 4.2 %fusion.31 = bf16[1024,256]{1,0:T(8,128)(2,1)S(1)} fusion(s32[256]{0:T(256)S(1)} %iota_add_fusion), kind=kLoop, calls=%fused_computation.50 | loop fusion | flops 4718592 | bytes 525312 | tf_op jit(solution)/shard_map/neg | solution.py:23
  125.6 1.1 pad_maximum_fusion
  126.7 80.5 %collective-permute-done.3 = bf16[1024,1024]{0,1:T(8,128)(2,1)} collective-permute-done((bf16[1024,1024]{0,1:T(8,128)(2,1)S(1)}, bf16[1024,1024]{0,1:T(8,128)(2,1)}, u32[]{:S(2)}, u32[]{:S(2)}) %collective-permute-start.3) | collective-permute-done | bytes 2097184 | tf_op jit(solution)/shard_map/ppermute | solution.py:78
  207.2 4.9 %maximum_select_fusion = bf16[1024,2048]{0,1:T(8,128)(2,1)} fusion(bf16[1024,1024]{0,1:T(8,128)(2,1)} %collective-permute-done.3, bf16[1024,1024]{0,1:T(8,128)(2,1)S(1)} %maximum_select_fusion.1, pred[]{:T(512)S(6)} %eq.50), kind=kLoop, calls=%fused_computation.26 | loop fusion | flops 18874368 | bytes 8388609 | tf_op jit(solution)/shard_map/jit(_where)/select_n | solution.py:81
  212.1 3.7 %gather_fusion = bf16[64,1024]{1,0:T(8,128)(2,1)S(1)} fusion(bf16[1024,2048]{0,1:T(8,128)(2,1)} %maximum_select_fusion, s32[1024]{0:T(1024)S(1)} %pad_clamp_fusion.1), kind=kCustom, calls=%fused_computation.clone | custom fusion | bytes 262400 | tf_op jit(solution)/shard_map/jit(_take)/gather | solution.py:87
  215.8 3.5 gather_fusion.1
  219.4 15.9 %while.10 = (s32[]{:T(128)}, bf16[2,32,64,256]{3,2,1,0:T(8,128)(2,1)S(1)}, f32[1024,64]{0,1:T(8,128)S(1)}, s32[2]{0:T(128)S(1)}, bf16[1024,64]{0,1:T(8,128)(2,1)...) while((s32[]{:T(128)}, ...), condition=%wide.region_3.5_spmd, body=%wide.region_2.4_spmd.sunk | while | flops 2181103616 | bytes 25297088 | solution.py:104
  219.5 0.6 dynamic_slice.15
  222.0 2.8 add_convert_fusion.2
  224.9 2.5 bitcast_dynamic-update-slice_fusion.2
  227.4 0.6 dynamic_slice.15
  230.0 2.8 add_convert_fusion.2
  232.8 2.5 bitcast_dynamic-update-slice_fusion.2
  235.4 1.3 copy-done.3
  236.9 33.0 %reduce-scatter.2.cloned.1.call-done = bf16[32,64,256]{2,1,0:T(8,128)(2,1)} async-done(((bf16[64,64,256]{2,1,0:T(8,128)(2,1)}), bf16[32,64,256]{2,1,0:T(8,128)(2,1)}) %reduce-scatter.2.cloned.1.call-update) | async-done | bytes 1048592 | tf_op jit(solution)/shard_map/reduce_scatter | solution.py:105
  269.9 1.6 fusion.18
  271.5 2.3 convert_bitcast_fusion
  273.8 1.8 copy.17
  275.6 76.3 %all_to_all.18 = bf16[192,1,32,256]{3,2,1,0:T(8,128)(2,1)S(1)} all-to-all(bf16[192,1,32,256]{3,2,1,0:T(8,128)(2,1)S(1)} %copy.17), channel_id=1, replica_groups=mesh['run'=1,'row'=16,'col'=1,'seg'=2] {'row'}, dimensions={0} | all-to-all | bytes 6291456 | tf_op jit(solution)/shard_map/all_to_all | solution.py:127
  352.0 2.1 copy.18
  (45 shorter events, 2.3 us)
Async XLA Ops:
  6.5 1.0 copy-start
  6.5 263.4 %reduce-scatter.2.cloned.1.call-start = ((), (), s32[]{:S(2)}) async-start(), calls=%async_computation.2 | async-start | bytes 3145728 | tf_op jit(solution)/shard_map/reduce_scatter | solution.py:105
  38.8 31.9 %copy-start.6 = (s32[64]{0:T(128)S(1)}, s32[64]{0:T(128)}, u32[]{:S(2)}) copy-start(s32[64]{0:T(128)} %param.9) | copy-start | bytes 772
  71.2 45.2 %copy-start.5 = (s32[64]{0:T(128)S(1)}, s32[64]{0:T(128)}, u32[]{:S(2)}) copy-start(s32[64]{0:T(128)} %param.10) | copy-start | bytes 772
  71.2 17.9 %copy-start.1 = (bf16[1024,2,64]{0,2,1:T(8,128)(2,1)}, bf16[1024,2,64]{0,2,1:T(8,128)(2,1)S(1)}, u32[]{:S(2)}) copy-start(bf16[1024,2,64]{0,2,1:T(8,128)(2,1)S(1)} %multiply_convert_fusion) | copy-start | bytes 786436
  71.3 1.6 collective-permute-start
  73.0 14.4 %collective-permute-start.1 = (bf16[1024,256]{0,1:T(8,128)(2,1)S(1)}, bf16[1024,256]{0,1:T(8,128)(2,1)S(1)}, u32[]{:S(2)}, u32[]{:S(2)}) collective-permute-start(bf16[1024,256]{0,1:T(8,128)(2,1)S(1)} %maximum_select_fusion.3), channel_id=1, source_target_pairs={{0,4},{2,6},{4,0},{6,2},{8,12},{10,14},{12,8},{14,10},{16,20},{18,... | collective-permute-start | bytes 1572872 | tf_op jit(solution)/shard_map/ppermute | solution.py:78
  87.8 23.9 %collective-permute-start.2 = (bf16[1024,512]{0,1:T(8,128)(2,1)S(1)}, bf16[1024,512]{0,1:T(8,128)(2,1)}, u32[]{:S(2)}, u32[]{:S(2)}) collective-permute-start(bf16[1024,512]{0,1:T(8,128)(2,1)S(1)} %maximum_select_fusion.2), channel_id=1, source_target_pairs={{0,8},{2,10},{4,12},{6,14},{8,0},{10,2},{12,4},{14,6},{16,24},{18,... | collective-permute-start | bytes 3145736 | tf_op jit(solution)/shard_map/ppermute | solution.py:78
  114.3 92.9 %collective-permute-start.3 = (bf16[1024,1024]{0,1:T(8,128)(2,1)S(1)}, bf16[1024,1024]{0,1:T(8,128)(2,1)}, u32[]{:S(2)}, u32[]{:S(2)}) collective-permute-start(bf16[1024,1024]{0,1:T(8,128)(2,1)S(1)} %maximum_select_fusion.1), channel_id=1, source_target_pairs={{0,16},{2,18},{4,20},{6,22},{8,24},{10,26},{12,28},{14,30},{16,0},... | collective-permute-start | bytes 6291464 | tf_op jit(solution)/shard_map/ppermute | solution.py:78
  212.1 7.3 %copy-start.2 = (bf16[2,32,64,256]{3,2,1,0:T(8,128)(2,1)S(1)}, bf16[2,32,64,256]{3,2,1,0:T(8,128)(2,1)}, u32[]{:S(2)}) copy-start(bf16[2,32,64,256]{3,2,1,0:T(8,128)(2,1)} %custom-call.4) | copy-start | bytes 6291460
  219.4 17.3 %copy-start.7 = (s32[64,1]{0,1:T(1,128)S(1)}, s32[64,1]{0,1:T(1,128)}, u32[]{:S(2)}) copy-start(s32[64,1]{0,1:T(1,128)} %param.11) | copy-start | bytes 772
  222.0 2.8 copy-start.4
  230.0 2.8 copy-start.4
  235.4 1.3 copy-start.3
Sparse Core Ops, SparseCore 0:
  236.8 33.0 reduce-scatter.1
